TPU v7x, 32 devices: a whole 2x2x4 slice. The times are simulated.
32 devices in a mesh: dp: 8 (over y, x, core), tp: 4 (over z).
Axes of the slice: x: 2, y: 2, z: 4, core: 2. Of those that a mesh axis runs over, the one named last changes fastest.
Arguments:
- tokens: bfloat16 [8, 512, 768], P('dp', 'tp'), may hold values from -6 to 6
- seg_ids: int32 [8, 512], P('dp'), may hold values from 0 to 2, never falling along the last dimension, each value on 1 to 256 neighbouring positions
- time_embed: float32 [8, 3, 768], P('dp'), may hold values from -6 to 6
- text_states: bfloat16 [8, 3, 64, 768], P('dp', None, 'tp'), may hold values from -6 to 6
- text_lengths: int32 [8, 3], P('dp'), may hold values from 16 to 64, as said below
- out_grad: bfloat16 [8, 512, 768], P('dp', 'tp'), may hold values from -6 to 6
- w_qkv: bfloat16 [768, 2304], P(None, 'tp'), may hold values from -0.21875 to 0.21875
- w_attn_out: bfloat16 [768, 768], P('tp'), may hold values from -3 to 3
- b_attn_out: bfloat16 [768], replicated, may hold values from -3 to 3
- w_cross_q: bfloat16 [768, 768], P(None, 'tp'), may hold values from -0.21875 to 0.21875
- w_cross_kv: bfloat16 [768, 1536], P(None, 'tp'), may hold values from -0.21875 to 0.21875
- w_cross_out: bfloat16 [768, 768], P('tp'), may hold values from -0.875 to 0.875
- b_cross_out: bfloat16 [768], replicated, may hold values from -3 to 3
- w_up: bfloat16 [768, 3072], P(None, 'tp'), may hold values from -0.21875 to 0.21875
- b_up: bfloat16 [3072], P('tp'), may hold values from -3 to 3
- w_down: bfloat16 [3072, 768], P('tp'), may hold values from -0.109375 to 0.109375
- w_mod: bfloat16 [768, 4608], P(None, 'tp'), may hold values from -0.21875 to 0.21875
- b_mod: bfloat16 [4608], P('tp'), may hold values from -3 to 3
Outputs:
- d_tokens: bfloat16 [8, 512, 768], P('dp', 'tp')
- d_time: float32 [8, 3, 768], P('dp')
- d_text: bfloat16 [8, 3, 64, 768], P('dp', None, 'tp')
- g_qkv: float32 [768, 2304], P(None, 'tp')
- g_attn_out: float32 [768, 768], P('tp')
- gb_attn_out: float32 [768], replicated
- g_cross_q: float32 [768, 768], P(None, 'tp')
- g_cross_kv: float32 [768, 1536], P(None, 'tp')
- g_cross_out: float32 [768, 768], P('tp')
- gb_cross_out: float32 [768], replicated
- g_up: float32 [768, 3072], P(None, 'tp')
- gb_up: float32 [3072], P('tp')
- g_down: float32 [3072, 768], P('tp')
- g_mod: float32 [768, 4608], P(None, 'tp')
- gb_mod: float32 [4608], P('tp')
Inputs may be any that keep to these rules, and one draw needn't show every extreme that they name: `seg_ids`: along a group's row item numbers never fall and every item of 0 to 2 has 1 to 256 frames. `text_lengths`: in every group one item has all 64 text tokens valid.
All inputs are finite; a program needn't handle non-finite values.
Results may differ from a plain program's by a relative error of at most 0.02.
Values may be sent and summed in bfloat16 or wider, within the bound.
A program may use at most 128 MiB of HBM per device.

v0:
```python
import math
import jax
import jax.numpy as jnp
from jax import lax
from jax.sharding import PartitionSpec as P

DH = 64


def dot_plain(left, right):
    return jnp.dot(left, right, preferred_element_type=jnp.float32)


def dot_left_t(left, right):
    return lax.dot_general(
        left, right, (((0,), (0,)), ((), ())), preferred_element_type=jnp.float32
    )


def dot_right_t(left, right):
    return lax.dot_general(
        left, right, (((1,), (1,)), ((), ())), preferred_element_type=jnp.float32
    )


def gelu_tanh(values):
    return jax.nn.gelu(values, approximate=True)


def normalize(values):
    center = values - jnp.mean(values, axis=-1, keepdims=True)
    inverse = lax.rsqrt(jnp.mean(center * center, axis=-1, keepdims=True) + 1e-06)
    return (center * inverse, inverse)


def normalize_back(grad, normed, inverse):
    return inverse * (
        grad
        - jnp.mean(grad, axis=-1, keepdims=True)
        - normed * jnp.mean(grad * normed, axis=-1, keepdims=True)
    )


def gather_rows(local_rows):
    return lax.all_gather(local_rows, "tp", axis=0, tiled=True)


def gather_grads(local_rows):
    return lax.all_gather(local_rows, "tp", axis=0, tiled=True)


def scatter_grads(full_rows):
    return lax.psum_scatter(full_rows, "tp", scatter_dimension=0, tiled=True)


def scatter_rows(attended, weight):
    return lax.psum_scatter(dot_plain(attended, weight), "tp", scatter_dimension=0, tiled=True)


def sum_bucket(first, second, third):
    return lax.psum((first, second, third), "dp")


def masked_scores(query_block, keys, tag_block, key_tag, scaling):
    scores = (
        jnp.einsum("rhd,khd->hrk", query_block, keys, preferred_element_type=jnp.float32) * scaling
    )
    return jnp.where((tag_block[:, None] == key_tag[None, :])[None], scores, -1000000000.0)


def attend_forward(query, keys, values, row_tag, key_tag, scaling):
    rows = query.shape[0]
    block_rows = min(512, rows)
    block_count = rows // block_rows

    def one_block(inputs):
        query_block, tag_block = inputs
        scores = masked_scores(query_block, keys, tag_block, key_tag, scaling)
        peak = jnp.max(scores, axis=-1, keepdims=True)
        exponent = jnp.exp(scores - peak)
        row_total = jnp.sum(exponent, axis=-1, keepdims=True)
        probs = (exponent / row_total).astype(jnp.bfloat16)
        result = jnp.einsum("hrk,khd->rhd", probs, values, preferred_element_type=jnp.float32)
        return (result, peak[..., 0] + jnp.log(row_total[..., 0]))

    result, log_total = lax.map(
        one_block,
        (
            query.reshape(block_count, block_rows, query.shape[1], query.shape[2]),
            row_tag.reshape(block_count, block_rows),
        ),
    )
    return (result.reshape(rows, -1), log_total)


def attend_backward(query, keys, values, row_tag, key_tag, scaling, log_total, d_result):
    rows = query.shape[0]
    block_rows = min(512, rows)
    block_count = rows // block_rows

    def one_block(carry, inputs):
        query_block, tag_block, total_block, grad_block = inputs
        scores = masked_scores(query_block, keys, tag_block, key_tag, scaling)
        probs = jnp.exp(scores - total_block[:, :, None])
        d_values = jnp.einsum(
            "hrk,rhd->khd",
            probs.astype(jnp.bfloat16),
            grad_block,
            preferred_element_type=jnp.float32,
        )
        d_probs = jnp.einsum("rhd,khd->hrk", grad_block, values, preferred_element_type=jnp.float32)
        d_scores = (probs * (d_probs - jnp.sum(probs * d_probs, axis=-1, keepdims=True))).astype(
            jnp.bfloat16
        )
        d_query = (
            jnp.einsum("hrk,khd->rhd", d_scores, keys, preferred_element_type=jnp.float32) * scaling
        )
        d_keys = (
            jnp.einsum("hrk,rhd->khd", d_scores, query_block, preferred_element_type=jnp.float32)
            * scaling
        )
        return ((carry[0] + d_keys, carry[1] + d_values), d_query)

    zeros = jnp.zeros(keys.shape, jnp.float32)
    shaped = (block_count, block_rows, query.shape[1], query.shape[2])
    (d_keys, d_values), d_query = lax.scan(
        one_block,
        (zeros, zeros),
        (
            query.reshape(shaped),
            row_tag.reshape(block_count, block_rows),
            log_total,
            d_result.reshape(shaped),
        ),
    )
    return (d_query.reshape(query.shape), d_keys, d_values)


def body(
    tokens,
    seg_ids,
    time_embed,
    text_states,
    text_lengths,
    out_grad,
    w_qkv,
    w_attn_out,
    b_attn_out,
    w_cross_q,
    w_cross_kv,
    w_cross_out,
    b_cross_out,
    w_up,
    b_up,
    w_down,
    w_mod,
    b_mod,
):
    shard_rows = tokens.shape[1]
    model_width = tokens.shape[2]
    item_count = time_embed.shape[1]
    scaling = 1.0 / math.sqrt(DH)
    heads_local = w_qkv.shape[1] // (3 * DH)
    tp_rank = lax.axis_index("tp")
    segment = seg_ids[0]
    frames = segment.shape[0]
    item_ids = jnp.arange(item_count, dtype=jnp.int32)
    local_segment = lax.dynamic_slice_in_dim(segment, tp_rank * shard_rows, shard_rows)
    onehot = (local_segment[:, None] == item_ids[None, :]).astype(jnp.float32)
    silu_time, silu_pull = jax.vjp(jax.nn.silu, time_embed[0])
    silu_low = silu_time.astype(jnp.bfloat16)
    mod_local = dot_plain(silu_low, w_mod) + b_mod.astype(jnp.float32)
    modulation = lax.all_gather(mod_local, "tp", axis=1, tiled=True)
    per_frame = jnp.dot(onehot, modulation, precision=lax.Precision.HIGHEST)
    shift_a, scale_a, gate_a, shift_m, scale_m, gate_m = jnp.split(per_frame, 6, axis=1)
    text_full = lax.all_gather(text_states[0], "tp", axis=1, tiled=True)
    text_count = text_full.shape[1]
    text_flat = text_full.reshape(item_count * text_count, model_width)
    key_index = jnp.arange(item_count * text_count, dtype=jnp.int32)
    key_item = key_index // text_count
    key_limit = jnp.sum(
        jnp.where(key_item[:, None] == item_ids[None, :], text_lengths[0][None, :], 0), axis=1
    )
    key_tag = jnp.where(key_index % text_count < key_limit, key_item, -1)
    stream_in = tokens[0].astype(jnp.float32)
    normed_a, inverse_a = normalize(stream_in)
    attn_in = gather_rows((normed_a * (1.0 + scale_a) + shift_a).astype(jnp.bfloat16))
    qkv = dot_plain(attn_in, w_qkv).astype(jnp.bfloat16).reshape(frames, heads_local, 3, DH)
    query, keys, values = (qkv[:, :, 0], qkv[:, :, 1], qkv[:, :, 2])
    attended, total_self = attend_forward(query, keys, values, segment, segment, scaling)
    attended = attended.astype(jnp.bfloat16)
    branch_a = scatter_rows(attended, w_attn_out) + b_attn_out.astype(jnp.float32)
    stream_a = stream_in + gate_a * branch_a
    normed_c, inverse_c = normalize(stream_a)
    cross_in = gather_rows(normed_c.astype(jnp.bfloat16))
    cross_query = (
        dot_plain(cross_in, w_cross_q).astype(jnp.bfloat16).reshape(frames, heads_local, DH)
    )
    cross_kv = (
        dot_plain(text_flat, w_cross_kv)
        .astype(jnp.bfloat16)
        .reshape(item_count * text_count, heads_local, 2, DH)
    )
    cross_keys, cross_values = (cross_kv[:, :, 0], cross_kv[:, :, 1])
    cross_attended, total_cross = attend_forward(
        cross_query, cross_keys, cross_values, segment, key_tag, scaling
    )
    cross_attended = cross_attended.astype(jnp.bfloat16)
    branch_c = scatter_rows(cross_attended, w_cross_out) + b_cross_out.astype(jnp.float32)
    stream_c = stream_a + branch_c
    normed_m, inverse_m = normalize(stream_c)
    mlp_in = gather_rows((normed_m * (1.0 + scale_m) + shift_m).astype(jnp.bfloat16))
    pre = dot_plain(mlp_in, w_up) + b_up.astype(jnp.float32)
    act, gelu_pull = jax.vjp(gelu_tanh, pre)
    act = act.astype(jnp.bfloat16)
    branch_m = scatter_rows(act, w_down)
    grad_out = out_grad[0].astype(jnp.float32)
    d_gate_m = grad_out * branch_m
    d_branch_m = gather_grads((grad_out * gate_m).astype(jnp.bfloat16))
    g_down = dot_left_t(act, d_branch_m)
    d_pre = gelu_pull(dot_right_t(d_branch_m, w_down))[0].astype(jnp.bfloat16)
    g_up = dot_left_t(mlp_in, d_pre)
    gb_up = jnp.sum(d_pre.astype(jnp.float32), axis=0)
    g_down, g_up, gb_up = sum_bucket(g_down, g_up, gb_up)
    d_mlp_in = scatter_grads(dot_right_t(d_pre, w_up))
    d_scale_m = d_mlp_in * normed_m
    grad_c = grad_out + normalize_back(d_mlp_in * (1.0 + scale_m), normed_m, inverse_m)
    d_branch_c = gather_grads(grad_c.astype(jnp.bfloat16))
    g_cross_out = dot_left_t(cross_attended, d_branch_c)
    gb_cross_out = jnp.sum(d_branch_c.astype(jnp.float32), axis=0)
    d_cross_result = (
        dot_right_t(d_branch_c, w_cross_out).astype(jnp.bfloat16).reshape(frames, heads_local, DH)
    )
    d_cross_query, d_cross_keys, d_cross_values = attend_backward(
        cross_query,
        cross_keys,
        cross_values,
        segment,
        key_tag,
        scaling,
        total_cross,
        d_cross_result,
    )
    d_cross_query = d_cross_query.reshape(frames, -1).astype(jnp.bfloat16)
    d_cross_kv = (
        jnp.stack([d_cross_keys, d_cross_values], axis=2)
        .reshape(item_count * text_count, -1)
        .astype(jnp.bfloat16)
    )
    g_cross_q = dot_left_t(cross_in, d_cross_query)
    g_cross_kv = dot_left_t(text_flat, d_cross_kv)
    g_cross_out, g_cross_q, g_cross_kv = sum_bucket(g_cross_out, g_cross_q, g_cross_kv)
    text_term = dot_right_t(d_cross_kv, w_cross_kv).reshape(item_count, text_count, model_width)
    d_text = lax.psum_scatter(text_term, "tp", scatter_dimension=1, tiled=True).astype(jnp.bfloat16)
    d_cross_in = scatter_grads(dot_right_t(d_cross_query, w_cross_q))
    grad_a = grad_c + normalize_back(d_cross_in, normed_c, inverse_c)
    d_gate_a = grad_a * branch_a
    d_branch_a = gather_grads((grad_a * gate_a).astype(jnp.bfloat16))
    g_attn_out = dot_left_t(attended, d_branch_a)
    gb_attn_out = jnp.sum(d_branch_a.astype(jnp.float32), axis=0)
    d_result = (
        dot_right_t(d_branch_a, w_attn_out).astype(jnp.bfloat16).reshape(frames, heads_local, DH)
    )
    d_query, d_keys, d_values = attend_backward(
        query, keys, values, segment, segment, scaling, total_self, d_result
    )
    d_qkv = jnp.stack([d_query, d_keys, d_values], axis=2).reshape(frames, -1).astype(jnp.bfloat16)
    g_qkv = dot_left_t(attn_in, d_qkv)
    g_attn_out, g_qkv, gb_attn_out = sum_bucket(g_attn_out, g_qkv, gb_attn_out)
    d_attn_in = scatter_grads(dot_right_t(d_qkv, w_qkv))
    d_scale_a = d_attn_in * normed_a
    d_tokens = (grad_a + normalize_back(d_attn_in * (1.0 + scale_a), normed_a, inverse_a)).astype(
        jnp.bfloat16
    )
    d_per_frame = jnp.concatenate(
        [d_attn_in, d_scale_a, d_gate_a, d_mlp_in, d_scale_m, d_gate_m], axis=1
    )
    d_mod_partial = jnp.dot(onehot.T, d_per_frame, precision=lax.Precision.HIGHEST)
    d_modulation = lax.psum_scatter(d_mod_partial, "tp", scatter_dimension=1, tiled=True).astype(
        jnp.bfloat16
    )
    g_mod = dot_left_t(silu_low, d_modulation)
    gb_mod = jnp.sum(d_modulation.astype(jnp.float32), axis=0)
    d_silu = lax.psum(dot_right_t(d_modulation, w_mod), "tp")
    d_time = silu_pull(d_silu)[0]
    g_mod, gb_mod, gb_cross_out = sum_bucket(g_mod, gb_mod, gb_cross_out)
    return (
        d_tokens[None],
        d_time[None],
        d_text[None],
        g_qkv,
        g_attn_out,
        gb_attn_out,
        g_cross_q,
        g_cross_kv,
        g_cross_out,
        gb_cross_out,
        g_up,
        gb_up,
        g_down,
        g_mod,
        gb_mod,
    )


def solution(mesh):
    placed = (
        P("dp", "tp", None),
        P("dp", None),
        P("dp", None, None),
        P("dp", None, "tp", None),
        P("dp", None),
        P("dp", "tp", None),
        P(None, "tp"),
        P("tp", None),
        P(),
        P(None, "tp"),
        P(None, "tp"),
        P("tp", None),
        P(),
        P(None, "tp"),
        P("tp"),
        P("tp", None),
        P(None, "tp"),
        P("tp"),
    )
    return jax.shard_map(
        body,
        mesh=mesh,
        in_specs=placed,
        out_specs=(
            P("dp", "tp", None),
            P("dp", None, None),
            P("dp", None, "tp", None),
            P(None, "tp"),
            P("tp", None),
            P(),
            P(None, "tp"),
            P(None, "tp"),
            P("tp", None),
            P(),
            P(None, "tp"),
            P("tp"),
            P("tp", None),
            P(None, "tp"),
            P("tp"),
        ),
        check_vma=False,
    )
```

profile of v0, /device:TPU:0, one launch (start us, length us, event | category | flops | bytes accessed | tf_op | source)
XLA Modules:
  0.0 679.7 jit_solution(6979725413255573108)
XLA Ops:
  11.3 15.1 %all_gather.24 = f32[3,4608]{1,0:T(4,128)S(1)} all-gather(f32[3,1152]{1,0:T(4,128)S(1)} %convolution_add_fusion), channel_id=1, replica_groups=mesh['dp'=8,'tp'=4] {'tp'}, dimensions={1}, use_global_device_ids=true | all-gather | bytes 69120 | tf_op jit(solution)/shard_map/all_gather | solution.py:173
  29.4 17.9 %all_gather.25 = bf16[512,768]{1,0:T(8,128)(2,1)S(1)} all-gather(bf16[128,768]{1,0:T(8,128)(2,1)S(1)} %fusion.42), channel_id=1, replica_groups=mesh['dp'=8,'tp'=4] {'tp'}, dimensions={0}, use_global_device_ids=true | all-gather | bytes 983040 | tf_op jit(solution)/shard_map/all_gather | solution.py:45
  53.7 15.6 %all-gather = bf16[1,3,64,768]{3,2,1,0:T(8,128)(2,1)S(1)} all-gather(bf16[1,3,16,768]{3,2,1,0:T(8,128)(2,1)S(1)} %copy-done.64), channel_id=2, replica_groups=mesh['dp'=8,'tp'=4] {'tp'}, dimensions={2}, use_global_device_ids=true | all-gather | bytes 368640 | tf_op jit(solution)/shard_map/all_gather | solution.py:176
  72.1 18.7 %reduce-scatter.11.cloned.1.call-done = f32[128,768]{1,0:T(8,128)} async-done(((f32[512,768]{1,0:T(8,128)}), f32[128,768]{1,0:T(8,128)}) %reduce-scatter.11.cloned.1.call-update) | async-done | bytes 393232 | tf_op jit(solution)/shard_map/reduce_scatter | solution.py:57
  92.4 17.6 %all_gather.27 = bf16[512,768]{1,0:T(8,128)(2,1)S(1)} all-gather(bf16[128,768]{1,0:T(8,128)(2,1)S(1)} %fusion.55), channel_id=1, replica_groups=mesh['dp'=8,'tp'=4] {'tp'}, dimensions={0}, use_global_device_ids=true | all-gather | bytes 983040 | tf_op jit(solution)/shard_map/all_gather | solution.py:45
  115.9 33.8 %reduce-scatter.13.cloned.1.call-done = f32[128,768]{1,0:T(8,128)} async-done(((f32[512,768]{1,0:T(8,128)}), f32[128,768]{1,0:T(8,128)}) %reduce-scatter.13.cloned.1.call-update) | async-done | bytes 393232 | tf_op jit(solution)/shard_map/reduce_scatter | solution.py:57
  152.6 18.2 %all_gather.28 = bf16[512,768]{1,0:T(8,128)(2,1)S(1)} all-gather(bf16[128,768]{1,0:T(8,128)(2,1)S(1)} %get-tuple-element.211), channel_id=1, replica_groups=mesh['dp'=8,'tp'=4] {'tp'}, dimensions={0}, use_global_device_ids=true | all-gather | bytes 983040 | tf_op jit(solution)/shard_map/all_gather | solution.py:49
  170.8 17.5 %all_gather.29 = bf16[512,768]{1,0:T(8,128)(2,1)S(1)} all-gather(bf16[128,768]{1,0:T(8,128)(2,1)S(1)} %get-tuple-element.212), channel_id=1, replica_groups=mesh['dp'=8,'tp'=4] {'tp'}, dimensions={0}, use_global_device_ids=true | all-gather | bytes 983040 | tf_op jit(solution)/shard_map/all_gather | solution.py:45
  189.9 3.4 convert_reduce_fusion
  196.9 34.3 %reduce-scatter.15.cloned.1.call-done = f32[128,768]{1,0:T(8,128)} async-done(((f32[512,768]{1,0:T(8,128)}), f32[128,768]{1,0:T(8,128)}) %reduce-scatter.15.cloned.1.call-update) | async-done | bytes 393232 | tf_op jit(solution)/shard_map/reduce_scatter | solution.py:53
  232.7 2.3 fusion.82
  235.0 18.5 %all_gather.30 = bf16[512,768]{1,0:T(8,128)(2,1)S(1)} all-gather(bf16[128,768]{1,0:T(8,128)(2,1)S(1)} %get-tuple-element.205), channel_id=1, replica_groups=mesh['dp'=8,'tp'=4] {'tp'}, dimensions={0}, use_global_device_ids=true | all-gather | bytes 983040 | tf_op jit(solution)/shard_map/all_gather | solution.py:49
  259.8 33.9 %reduce-scatter.17.cloned.1.call-done = f32[128,768]{1,0:T(8,128)} async-done(((f32[512,768]{1,0:T(8,128)}), f32[128,768]{1,0:T(8,128)}) %reduce-scatter.17.cloned.1.call-update) | async-done | bytes 393232 | tf_op jit(solution)/shard_map/reduce_scatter | solution.py:53
  295.0 2.3 multiply_convert_fusion.3
  297.4 18.1 %all_gather.31 = bf16[512,768]{1,0:T(8,128)(2,1)S(1)} all-gather(bf16[128,768]{1,0:T(8,128)(2,1)S(1)} %get-tuple-element.203), channel_id=1, replica_groups=mesh['dp'=8,'tp'=4] {'tp'}, dimensions={0}, use_global_device_ids=true | all-gather | bytes 983040 | tf_op jit(solution)/shard_map/all_gather | solution.py:49
  323.9 4.0 fusion.79
  328.0 3.9 fusion.96
  331.9 2.4 fusion.78
  337.8 20.7 %reduce-scatter.19.cloned.1.call-done = f32[128,768]{1,0:T(8,128)} async-done(((f32[512,768]{1,0:T(8,128)}), f32[128,768]{1,0:T(8,128)}) %reduce-scatter.19.cloned.1.call-update) | async-done | bytes 393232 | tf_op jit(solution)/shard_map/reduce_scatter | solution.py:53
  358.6 2.0 fusion.77
  360.6 2.1 fusion.48
  365.1 30.4 %reduce-scatter.21.cloned.1.call-done = f32[128,768]{1,0:T(8,128)} async-done(((f32[512,768]{1,0:T(8,128)}), f32[128,768]{1,0:T(8,128)}) %reduce-scatter.21.cloned.1.call-update) | async-done | bytes 393232 | tf_op jit(solution)/shard_map/reduce_scatter | solution.py:57
  397.3 5.1 convolution_bitcast_fusion
  404.8 2.5 fusion.98
  411.7 38.0 %reduce-scatter.25.cloned.1.call-done = f32[1152,3]{1,0:T(8,128)} async-done(((f32[4608,3]{1,0:T(8,128)}), f32[1152,3]{1,0:T(8,128)}) %reduce-scatter.25.cloned.1.call-update) | async-done | bytes 13840
  450.9 2.5 fusion.70
  453.6 20.4 %reduce-scatter.23.cloned.1.call-done = f32[3,16,768]{2,1,0:T(8,128)} async-done(((f32[3,64,768]{2,1,0:T(8,128)}), f32[3,16,768]{2,1,0:T(8,128)}) %reduce-scatter.23.cloned.1.call-update) | async-done | bytes 147472 | tf_op jit(solution)/shard_map/reduce_scatter | solution.py:254
  476.3 16.1 %psum.91 = f32[3,768]{1,0:T(4,128)S(1)} all-reduce(f32[3,768]{1,0:T(4,128)S(1)} %fusion.99), channel_id=1, replica_groups=mesh['dp'=8,'tp'=4] {'tp'}, use_global_device_ids=true, to_apply=%region_26.27 | all-reduce | flops 2304 | bytes 18432 | tf_op jit(solution)/shard_map/psum | solution.py:284
  493.1 24.7 %all-reduce = (f32[768]{0:T(1024)}, f32[768]{0:T(1024)}, f32[768]{0:T(1024)}, f32[1152]{0:T(1024)}) all-reduce(f32[768]{0:T(1024)S(1)} %convert_reduce_fusion.2, f32[768]{0:T(1024)S(1)} %convert_reduce_fusion.1, f32[768]{0:T(1024)S(1)} %copy-done.81, f32[1152]{0:T(1024)S(1)} %convert_reduce_fusion.4), channel_id=1, replica_groups=mesh['dp'=8,'tp'=4] {'dp'}, use_global_device_ids=true, to_apply=%region_31.32 | all-reduce | flops 3456 | bytes 27648 | tf_op jit(solution)/shard_map/psum | solution.py:61
  517.8 140.2 %all-reduce.4.cloned.1.call-done = (f32[768,576]{0,1:T(8,128)}, f32[192,768]{1,0:T(8,128)}, f32[768,192]{0,1:T(8,128)}, f32[768,384]{0,1:T(8,128)}, f32[192,768]...) async-done(((f32[768,576]{0,1:T(8,128)}, f32[192,768]{1,0:T(8,128)}, f32[768,192]{0,1:T(8,128)}, f32[768,384]{0,1:T(8,128)}, ...) | async-done | bytes 12976144 | tf_op jit(solution)/shard_map/psum | solution.py:61
  658.0 2.7 copy.88
  660.6 2.9 copy.133
  (293 shorter events, 77.2 us)
Async XLA Ops:
  7.2 19.2 %copy-start.70 = (s32[1,512]{1,0:T(1,128)S(1)}, s32[1,512]{1,0:T(1,128)}, u32[]{:S(2)}) copy-start(s32[1,512]{1,0:T(1,128)} %param.19) | copy-start | bytes 6148
  7.2 83.6 %reduce-scatter.11.cloned.1.call-start = ((), (), s32[]{:S(2)}) async-start(), calls=%async_computation.8 | async-start | bytes 1966080 | tf_op jit(solution)/shard_map/reduce_scatter | solution.py:57
  8.4 19.3 %copy-start.73 = (f32[128]{0:T(128)}, f32[128]{0:T(128)S(1)}, u32[]{:S(2)}) copy-start(f32[128]{0:T(128)S(1)} %broadcast_multiply_fusion.8) | copy-start | bytes 1540
  53.6 96.1 %reduce-scatter.13.cloned.1.call-start = ((), (), s32[]{:S(2)}) async-start(), calls=%async_computation.9 | async-start | bytes 1966080 | tf_op jit(solution)/shard_map/reduce_scatter | solution.py:57
  53.7 38.3 %copy-start.65 = (f32[768]{0:T(1024)}, f32[768]{0:T(1024)S(1)}, u32[]{:S(2)}) copy-start(f32[768]{0:T(1024)S(1)} %convert_element_type.171) | copy-start | bytes 9220
  72.1 37.9 %copy-start.43 = (bf16[768,192]{0,1:T(8,128)(2,1)S(1)}, bf16[768,192]{0,1:T(8,128)(2,1)}, u32[]{:S(2)}) copy-start(bf16[768,192]{0,1:T(8,128)(2,1)} %param.27) | copy-start | bytes 884740
  92.1 19.0 %copy-start.39 = (bf16[192,384]{0,1:T(8,128)(2,1)S(1)}, bf16[192,384]{0,1:T(8,128)(2,1)}, u32[]{:S(2)}) copy-start(bf16[192,384]{0,1:T(8,128)(2,1)} %copy.78) | copy-start | bytes 442372
  92.3 19.2 %copy-start.80 = (f32[128]{0:T(128)}, f32[128]{0:T(128)S(1)}, u32[]{:S(2)}) copy-start(f32[128]{0:T(128)S(1)} %add_rsqrt_fusion.1) | copy-start | bytes 1540
  114.6 116.6 %reduce-scatter.15.cloned.1.call-start = ((), (), s32[]{:S(2)}) async-start(), calls=%async_computation.10 | async-start | bytes 1966080 | tf_op jit(solution)/shard_map/reduce_scatter | solution.py:53
  150.8 19.9 %copy-start.4 = (f32[128,768]{1,0:T(8,128)}, f32[128,768]{1,0:T(8,128)S(1)}, u32[]{:S(2)}) copy-start(f32[128,768]{1,0:T(8,128)S(1)} %get-tuple-element.208) | copy-start | bytes 1179652
  150.9 19.9 %copy-start.71 = (f32[128]{0:T(128)}, f32[128]{0:T(128)S(1)}, u32[]{:S(2)}) copy-start(f32[128]{0:T(128)S(1)} %broadcast_multiply_fusion.6) | copy-start | bytes 1540
  151.1 19.7 %copy-start.76 = (f32[128]{0:T(128)}, f32[128]{0:T(128)S(1)}, u32[]{:S(2)}) copy-start(f32[128]{0:T(128)S(1)} %add_rsqrt_fusion) | copy-start | bytes 1540
  151.1 37.2 %copy-start.89 = (bf16[768,768]{1,0:T(8,128)(2,1)S(1)}, bf16[768,768]{1,0:T(8,128)(2,1)}, u32[]{:S(2)}) copy-start(bf16[768,768]{1,0:T(8,128)(2,1)} %param.33) | copy-start | bytes 3538948
  196.2 97.6 %reduce-scatter.17.cloned.1.call-start = ((), (), s32[]{:S(2)}) async-start(), calls=%async_computation.11 | async-start | bytes 1966080 | tf_op jit(solution)/shard_map/reduce_scatter | solution.py:53
  232.6 21.7 %copy-start.42 = (bf16[192,768]{1,0:T(8,128)(2,1)S(1)}, bf16[192,768]{1,0:T(8,128)(2,1)}, u32[]{:S(2)}) copy-start(bf16[192,768]{1,0:T(8,128)(2,1)} %param.29) | copy-start | bytes 884740
  235.0 19.8 %copy-start.40 = (bf16[192,384]{0,1:T(8,128)(2,1)S(1)}, bf16[192,384]{0,1:T(8,128)(2,1)}, u32[]{:S(2)}) copy-start(bf16[192,384]{0,1:T(8,128)(2,1)} %copy.78) | copy-start | bytes 442372
  259.0 99.5 %reduce-scatter.19.cloned.1.call-start = ((), (), s32[]{:S(2)}) async-start(), calls=%async_computation.12 | async-start | bytes 1966080 | tf_op jit(solution)/shard_map/reduce_scatter | solution.py:53
  293.8 22.7 %copy-start.46 = (bf16[192,768]{1,0:T(8,128)(2,1)S(1)}, bf16[192,768]{1,0:T(8,128)(2,1)}, u32[]{:S(2)}) copy-start(bf16[192,768]{1,0:T(8,128)(2,1)} %param.25) | copy-start | bytes 884740
  295.0 21.8 %copy-start.2 = (f32[3,512,512]{1,2,0:T(8,128)S(1)}, f32[3,512,512]{1,2,0:T(8,128)}, u32[]{:S(2)}) copy-start(f32[3,512,512]{1,2,0:T(8,128)} %copy-done.1) | copy-start | bytes 9437188
  323.9 71.7 %reduce-scatter.21.cloned.1.call-start = ((), (), s32[]{:S(2)}) async-start(), calls=%async_computation.13 | async-start | bytes 1966080 | tf_op jit(solution)/shard_map/reduce_scatter | solution.py:57
  327.9 121.8 %reduce-scatter.25.cloned.1.call-start = ((), (), s32[]{:S(2)}) async-start(), calls=%async_computation.15 | async-start | bytes 2949120
  335.0 23.5 %copy-start.74 = (f32[128]{0:T(128)S(1)}, f32[128]{0:T(128)}, u32[]{:S(2)}) copy-start(f32[128]{0:T(128)} %copy-done.73) | copy-start | bytes 1540
  335.0 23.5 %copy-start.79 = (f32[128]{0:T(128)S(1)}, f32[128]{0:T(128)}, u32[]{:S(2)}) copy-start(f32[128]{0:T(128)} %copy-done.78) | copy-start | bytes 1540
  336.6 23.9 %copy-start.19 = (f32[128,768]{1,0:T(8,128)S(1)}, f32[128,768]{1,0:T(8,128)}, u32[]{:S(2)}) copy-start(f32[128,768]{1,0:T(8,128)} %get-tuple-element.204) | copy-start | bytes 1179652
  337.8 24.9 %copy-start.37 = (f32[128,768]{1,0:T(8,128)S(1)}, f32[128,768]{1,0:T(8,128)}, u32[]{:S(2)}) copy-start(f32[128,768]{1,0:T(8,128)} %reduce-scatter.11.cloned.1.call-done) | copy-start | bytes 1179652
  337.8 24.9 %copy-start.66 = (f32[768]{0:T(1024)S(1)}, f32[768]{0:T(1024)}, u32[]{:S(2)}) copy-start(f32[768]{0:T(1024)} %copy-done.65) | copy-start | bytes 9220
  362.7 32.9 %copy-start.34 = (bf16[1,128,768]{2,1,0:T(8,128)(2,1)S(1)}, bf16[1,128,768]{2,1,0:T(8,128)(2,1)}, u32[]{:S(2)}) copy-start(bf16[1,128,768]{2,1,0:T(8,128)(2,1)} %param.23) | copy-start | bytes 589828
  363.5 33.9 %copy-start.86 = (s32[128]{0:T(128)S(1)}, s32[128]{0:T(128)}, u32[]{:S(2)}) copy-start(s32[128]{0:T(128)} %copy-done.85) | copy-start | bytes 1540
  402.5 71.5 %reduce-scatter.23.cloned.1.call-start = ((), (), s32[]{:S(2)}) async-start(), calls=%async_computation.14 | async-start | bytes 737280 | tf_op jit(solution)/shard_map/reduce_scatter | solution.py:254
  404.8 253.2 %all-reduce.4.cloned.1.call-start = ((), (), s32[]{:S(2)}) async-start(), calls=%async_computation.16 | async-start | bytes 25952256 | tf_op jit(solution)/shard_map/psum | solution.py:61
  409.8 41.1 %copy-start.63 = (f32[1,3,768]{2,0,1:T(1,128)S(1)}, f32[1,3,768]{2,0,1:T(1,128)}, u32[]{:S(2)}) copy-start(f32[1,3,768]{2,0,1:T(1,128)} %param.20) | copy-start | bytes 27652
  453.6 39.5 %copy-start.81 = (f32[768]{0:T(1024)S(1)}, f32[768]{0:T(1024)}, u32[]{:S(2)}) copy-start(f32[768]{0:T(1024)} %get-tuple-element.201) | copy-start | bytes 9220
  (68 other events, 262.3 us)
Sparse Core Ops, SparseCore 0:
  53.7 36.9 reduce-scatter.10
  114.7 34.9 reduce-scatter.12
  196.3 34.8 reduce-scatter.14
  259.2 34.5 reduce-scatter.16
  324.0 34.5 reduce-scatter.18
  361.3 34.2 reduce-scatter.20
  402.6 46.9 reduce-scatter.24
  452.5 21.4 reduce-scatter.22
  480.0 177.9 all-reduce.3
where the time goes:
time: 681 us; the launch traced here: 680 us
  waiting for transfers between devices  371 us (54%)
  blocking collectives  179 us (26%)
  matrix products  50.5 us (7%)
  local copies, waits for them, and re-layouts  34 us (5%)
  other arithmetic  30 us (4%)
  between operations  14.7 us (2%)
    psum x1, waiting for transfers between devices, sum_bucket(): return lax.psum((first, second, third), 'dp')  140 us
    reduce_scatter x3, waiting for transfers between devices, scatter_grads(): return lax.psum_scatter(full_rows, 'tp', scatter_dimension=0, tiled=True)  89 us
    reduce_scatter x3, waiting for transfers between devices, scatter_rows(): lax.psum_scatter(dot_plain(attended, weight), 'tp', scatter_dimension=0,...  82.9 us
    all_gather x3, blocking collectives, gather_grads(): return lax.all_gather(local_rows, 'tp', axis=0, tiled=True)  54.7 us
    all_gather x3, blocking collectives, gather_rows(): return lax.all_gather(local_rows, 'tp', axis=0, tiled=True)  53 us
    unnamed x10, waiting for transfers between devices  38.1 us
    unnamed x193, local copies, waits for them, and re-layouts  32.1 us
    psum x1, blocking collectives, sum_bucket(): return lax.psum((first, second, third), 'dp')  24.7 us
  transfers between devices with their start and end apart: 9, of which 9 were waited for; matrix products, arithmetic and copies ran while one was open for 6% of the time, Pallas kernels for 0%

commit v1 on v0

--- a/solution.py
+++ b/solution.py
@@ -5,6 +5,27 @@
 from jax.sharding import PartitionSpec as P
 
 DH = 64
+
+
+def ring_gather(x, axis, dim):
+    size, position, rows = (lax.axis_size(axis), lax.axis_index(axis), x.shape[dim])
+    right = [(i, (i + 1) % size) for i in range(size)]
+    behind = [(i, (i - 1) % size) for i in range(size)]
+    out = jnp.zeros((*x.shape[:dim], size * rows, *x.shape[dim + 1 :]), x.dtype)
+    out = lax.dynamic_update_slice_in_dim(out, x, position * rows, axis=dim)
+    from_left = from_right = x
+    half = size // 2
+    for step in range(1, half + 1):
+        from_left = lax.ppermute(from_left, axis, right)
+        out = lax.dynamic_update_slice_in_dim(
+            out, from_left, (position - step) % size * rows, axis=dim
+        )
+        if step < size - half:
+            from_right = lax.ppermute(from_right, axis, behind)
+            out = lax.dynamic_update_slice_in_dim(
+                out, from_right, (position + step) % size * rows, axis=dim
+            )
+    return out
 
 
 def dot_plain(left, right):
@@ -173,7 +194,7 @@
     modulation = lax.all_gather(mod_local, "tp", axis=1, tiled=True)
     per_frame = jnp.dot(onehot, modulation, precision=lax.Precision.HIGHEST)
     shift_a, scale_a, gate_a, shift_m, scale_m, gate_m = jnp.split(per_frame, 6, axis=1)
-    text_full = lax.all_gather(text_states[0], "tp", axis=1, tiled=True)
+    text_full = ring_gather(text_states[0], "tp", 1)
     text_count = text_full.shape[1]
     text_flat = text_full.reshape(item_count * text_count, model_width)
     key_index = jnp.arange(item_count * text_count, dtype=jnp.int32)

time: 681 us -> 679 us (level)
  blocking collectives: 179 us -> 164 us
  waiting for transfers between devices: 371 us -> 382 us
    all_gather x1 -> x0, blocking collectives: 15.6 us -> none  [body(): text_full = lax.all_gather(text_states[0], 'tp', axis=1, tiled=True)]
    ppermute x0 -> x3, waiting for transfers between devices: none -> 9.05 us  [the longest x2 9.04 us: ring_gather(): from_left = lax.ppermute(from_left, axis, right)]
    unnamed x193 -> x195, local copies, waits for them, and re-layouts: 32.1 us -> 30.1 us
  transfers between devices with their start and end apart: 9 -> 12, of which waited for: 9 -> 11; matrix products, arithmetic and copies ran while one was open for 6% -> 6% of each run, Pallas kernels for 0% -> 0%
where the time goes in v1:
time: 679 us; the launch traced here: 678 us
  waiting for transfers between devices  382 us (56%)
  blocking collectives  164 us (24%)
  matrix products  50.5 us (7%)
  local copies, waits for them, and re-layouts  32.2 us (5%)
  other arithmetic  30 us (4%)
  between operations  14.8 us (2%)
    psum x1, waiting for transfers between devices, sum_bucket(): return lax.psum((first, second, third), 'dp')  140 us
    reduce_scatter x3, waiting for transfers between devices, scatter_grads(): return lax.psum_scatter(full_rows, 'tp', scatter_dimension=0, tiled=True)  89.1 us
    reduce_scatter x3, waiting for transfers between devices, scatter_rows(): lax.psum_scatter(dot_plain(attended, weight), 'tp', scatter_dimension=0,...  84.8 us
    all_gather x3, blocking collectives, gather_grads(): return lax.all_gather(local_rows, 'tp', axis=0, tiled=True)  54.6 us
    all_gather x3, blocking collectives, gather_rows(): return lax.all_gather(local_rows, 'tp', axis=0, tiled=True)  53.6 us
    unnamed x10, waiting for transfers between devices  38 us
    unnamed x195, local copies, waits for them, and re-layouts  30.1 us
    psum x1, blocking collectives, sum_bucket(): return lax.psum((first, second, third), 'dp')  24.7 us
  transfers between devices with their start and end apart: 12, of which 11 were waited for; matrix products, arithmetic and copies ran while one was open for 6% of the time, Pallas kernels for 0%

profile of v1, /device:TPU:0, one launch (start us, length us, event | category | flops | bytes accessed | tf_op | source)
XLA Modules:
  0.0 677.8 jit_solution(13343750505361217308)
XLA Ops:
  11.3 15.1 %all_gather.21 = f32[3,4608]{1,0:T(4,128)S(1)} all-gather(f32[3,1152]{1,0:T(4,128)S(1)} %convolution_add_fusion), channel_id=1, replica_groups=mesh['dp'=8,'tp'=4] {'tp'}, dimensions={1}, use_global_device_ids=true | all-gather | bytes 69120 | tf_op jit(solution)/shard_map/all_gather | solution.py:194
  29.4 17.9 %all_gather.22 = bf16[512,768]{1,0:T(8,128)(2,1)S(1)} all-gather(bf16[128,768]{1,0:T(8,128)(2,1)S(1)} %fusion.42), channel_id=1, replica_groups=mesh['dp'=8,'tp'=4] {'tp'}, dimensions={0}, use_global_device_ids=true | all-gather | bytes 983040 | tf_op jit(solution)/shard_map/all_gather | solution.py:66
  53.9 3.6 collective-permute-start.1
  60.0 7.6 %collective-permute-done.2 = bf16[3,16,768]{2,1,0:T(8,128)(2,1)S(1)} collective-permute-done((bf16[3,16,768]{2,1,0:T(8,128)(2,1)S(1)}, bf16[3,16,768]{2,1,0:T(8,128)(2,1)S(1)}, u32[]{:S(2)}, u32[]{:S(2)}) %collective-permute-start.2) | collective-permute-done | bytes 73760 | tf_op jit(solution)/shard_map/ppermute | solution.py:19
  68.7 21.0 %reduce-scatter.11.cloned.1.call-done = f32[128,768]{1,0:T(8,128)} async-done(((f32[512,768]{1,0:T(8,128)}), f32[128,768]{1,0:T(8,128)}) %reduce-scatter.11.cloned.1.call-update) | async-done | bytes 393232 | tf_op jit(solution)/shard_map/reduce_scatter | solution.py:78
  91.4 18.1 %all_gather.23 = bf16[512,768]{1,0:T(8,128)(2,1)S(1)} all-gather(bf16[128,768]{1,0:T(8,128)(2,1)S(1)} %fusion.55), channel_id=1, replica_groups=mesh['dp'=8,'tp'=4] {'tp'}, dimensions={0}, use_global_device_ids=true | all-gather | bytes 983040 | tf_op jit(solution)/shard_map/all_gather | solution.py:66
  115.5 33.4 %reduce-scatter.13.cloned.1.call-done = f32[128,768]{1,0:T(8,128)} async-done(((f32[512,768]{1,0:T(8,128)}), f32[128,768]{1,0:T(8,128)}) %reduce-scatter.13.cloned.1.call-update) | async-done | bytes 393232 | tf_op jit(solution)/shard_map/reduce_scatter | solution.py:78
  151.8 18.2 %all_gather.24 = bf16[512,768]{1,0:T(8,128)(2,1)S(1)} all-gather(bf16[128,768]{1,0:T(8,128)(2,1)S(1)} %get-tuple-element.211), channel_id=1, replica_groups=mesh['dp'=8,'tp'=4] {'tp'}, dimensions={0}, use_global_device_ids=true | all-gather | bytes 983040 | tf_op jit(solution)/shard_map/all_gather | solution.py:70
  170.0 17.5 %all_gather.25 = bf16[512,768]{1,0:T(8,128)(2,1)S(1)} all-gather(bf16[128,768]{1,0:T(8,128)(2,1)S(1)} %get-tuple-element.212), channel_id=1, replica_groups=mesh['dp'=8,'tp'=4] {'tp'}, dimensions={0}, use_global_device_ids=true | all-gather | bytes 983040 | tf_op jit(solution)/shard_map/all_gather | solution.py:66
  189.1 3.4 convert_reduce_fusion
  196.1 34.3 %reduce-scatter.15.cloned.1.call-done = f32[128,768]{1,0:T(8,128)} async-done(((f32[512,768]{1,0:T(8,128)}), f32[128,768]{1,0:T(8,128)}) %reduce-scatter.15.cloned.1.call-update) | async-done | bytes 393232 | tf_op jit(solution)/shard_map/reduce_scatter | solution.py:74
  231.8 2.3 fusion.83
  234.1 18.4 %all_gather.26 = bf16[512,768]{1,0:T(8,128)(2,1)S(1)} all-gather(bf16[128,768]{1,0:T(8,128)(2,1)S(1)} %get-tuple-element.205), channel_id=1, replica_groups=mesh['dp'=8,'tp'=4] {'tp'}, dimensions={0}, use_global_device_ids=true | all-gather | bytes 983040 | tf_op jit(solution)/shard_map/all_gather | solution.py:70
  258.8 34.1 %reduce-scatter.17.cloned.1.call-done = f32[128,768]{1,0:T(8,128)} async-done(((f32[512,768]{1,0:T(8,128)}), f32[128,768]{1,0:T(8,128)}) %reduce-scatter.17.cloned.1.call-update) | async-done | bytes 393232 | tf_op jit(solution)/shard_map/reduce_scatter | solution.py:74
  294.2 2.3 multiply_convert_fusion.3
  296.5 18.1 %all_gather.27 = bf16[512,768]{1,0:T(8,128)(2,1)S(1)} all-gather(bf16[128,768]{1,0:T(8,128)(2,1)S(1)} %get-tuple-element.203), channel_id=1, replica_groups=mesh['dp'=8,'tp'=4] {'tp'}, dimensions={0}, use_global_device_ids=true | all-gather | bytes 983040 | tf_op jit(solution)/shard_map/all_gather | solution.py:70
  323.0 4.0 fusion.80
  327.1 3.9 fusion.98
  331.1 2.4 fusion.79
  336.9 20.8 %reduce-scatter.19.cloned.1.call-done = f32[128,768]{1,0:T(8,128)} async-done(((f32[512,768]{1,0:T(8,128)}), f32[128,768]{1,0:T(8,128)}) %reduce-scatter.19.cloned.1.call-update) | async-done | bytes 393232 | tf_op jit(solution)/shard_map/reduce_scatter | solution.py:74
  357.7 2.0 fusion.78
  359.8 2.1 fusion.48
  364.3 30.4 %reduce-scatter.21.cloned.1.call-done = f32[128,768]{1,0:T(8,128)} async-done(((f32[512,768]{1,0:T(8,128)}), f32[128,768]{1,0:T(8,128)}) %reduce-scatter.21.cloned.1.call-update) | async-done | bytes 393232 | tf_op jit(solution)/shard_map/reduce_scatter | solution.py:78
  396.5 5.1 convolution_bitcast_fusion
  404.0 2.5 fusion.100
  410.9 37.9 %reduce-scatter.25.cloned.1.call-done = f32[1152,3]{1,0:T(8,128)} async-done(((f32[4608,3]{1,0:T(8,128)}), f32[1152,3]{1,0:T(8,128)}) %reduce-scatter.25.cloned.1.call-update) | async-done | bytes 13840
  450.1 2.5 fusion.71
  452.8 20.3 %reduce-scatter.23.cloned.1.call-done = f32[3,16,768]{2,1,0:T(8,128)} async-done(((f32[3,64,768]{2,1,0:T(8,128)}), f32[3,16,768]{2,1,0:T(8,128)}) %reduce-scatter.23.cloned.1.call-update) | async-done | bytes 147472 | tf_op jit(solution)/shard_map/reduce_scatter | solution.py:275
  475.3 16.2 %psum.91 = f32[3,768]{1,0:T(4,128)S(1)} all-reduce(f32[3,768]{1,0:T(4,128)S(1)} %fusion.101), channel_id=1, replica_groups=mesh['dp'=8,'tp'=4] {'tp'}, use_global_device_ids=true, to_apply=%region_26.27 | all-reduce | flops 2304 | bytes 18432 | tf_op jit(solution)/shard_map/psum | solution.py:305
  492.2 24.7 %all-reduce = (f32[768]{0:T(1024)}, f32[768]{0:T(1024)}, f32[768]{0:T(1024)}, f32[1152]{0:T(1024)}) all-reduce(f32[768]{0:T(1024)S(1)} %convert_reduce_fusion.2, f32[768]{0:T(1024)S(1)} %convert_reduce_fusion.1, f32[768]{0:T(1024)S(1)} %copy-done.82, f32[1152]{0:T(1024)S(1)} %convert_reduce_fusion.4), channel_id=1, replica_groups=mesh['dp'=8,'tp'=4] {'dp'}, use_global_device_ids=true, to_apply=%region_31.32 | all-reduce | flops 3456 | bytes 27648 | tf_op jit(solution)/shard_map/psum | solution.py:82
  516.9 140.2 %all-reduce.4.cloned.1.call-done = (f32[768,576]{0,1:T(8,128)}, f32[192,768]{1,0:T(8,128)}, f32[768,192]{0,1:T(8,128)}, f32[768,384]{1,0:T(8,128)}, f32[192,768]...) async-done(((f32[768,576]{0,1:T(8,128)}, f32[192,768]{1,0:T(8,128)}, f32[768,192]{0,1:T(8,128)}, f32[768,384]{1,0:T(8,128)}, ...) | async-done | bytes 12976144 | tf_op jit(solution)/shard_map/psum | solution.py:82
  657.2 2.9 copy.133
  (305 shorter events, 79.8 us)
Async XLA Ops:
  7.2 82.6 %reduce-scatter.11.cloned.1.call-start = ((), (), s32[]{:S(2)}) async-start(), calls=%async_computation.8 | async-start | bytes 1966080 | tf_op jit(solution)/shard_map/reduce_scatter | solution.py:78
  53.6 95.3 %reduce-scatter.13.cloned.1.call-start = ((), (), s32[]{:S(2)}) async-start(), calls=%async_computation.9 | async-start | bytes 1966080 | tf_op jit(solution)/shard_map/reduce_scatter | solution.py:78
  53.6 6.3 collective-permute-start
  53.9 6.0 collective-permute-start.1
  58.4 32.6 %copy-start.66 = (f32[768]{0:T(1024)}, f32[768]{0:T(1024)S(1)}, u32[]{:S(2)}) copy-start(f32[768]{0:T(1024)S(1)} %convert_element_type.171) | copy-start | bytes 9220
  59.9 7.6 %collective-permute-start.2 = (bf16[3,16,768]{2,1,0:T(8,128)(2,1)S(1)}, bf16[3,16,768]{2,1,0:T(8,128)(2,1)S(1)}, u32[]{:S(2)}, u32[]{:S(2)}) collective-permute-start(bf16[3,16,768]{2,1,0:T(8,128)(2,1)S(1)} %collective-permute-done), channel_id=1, source_target_pairs={{0,1},{1,2},{2,3},{3,0},{4,5},{5,6},{6,7},{7,4},{8,9},{9,10},{10,1... | collective-permute-start | bytes 221192 | tf_op jit(solution)/shard_map/ppermute | solution.py:19
  67.6 23.7 %copy-start.22 = (bf16[3,64,768]{2,1,0:T(8,128)(2,1)}, bf16[3,64,768]{2,1,0:T(8,128)(2,1)S(1)}, u32[]{:S(2)}) copy-start(bf16[3,64,768]{2,1,0:T(8,128)(2,1)S(1)} %constant_dynamic-update-slice_fusion.2) | copy-start | bytes 884740
  68.7 40.8 %copy-start.44 = (bf16[768,192]{0,1:T(8,128)(2,1)S(1)}, bf16[768,192]{0,1:T(8,128)(2,1)}, u32[]{:S(2)}) copy-start(bf16[768,192]{0,1:T(8,128)(2,1)} %param.27) | copy-start | bytes 884740
  114.1 116.2 %reduce-scatter.15.cloned.1.call-start = ((), (), s32[]{:S(2)}) async-start(), calls=%async_computation.10 | async-start | bytes 1966080 | tf_op jit(solution)/shard_map/reduce_scatter | solution.py:74
  150.0 19.9 %copy-start.4 = (f32[128,768]{1,0:T(8,128)}, f32[128,768]{1,0:T(8,128)S(1)}, u32[]{:S(2)}) copy-start(f32[128,768]{1,0:T(8,128)S(1)} %get-tuple-element.208) | copy-start | bytes 1179652
  150.0 19.9 %copy-start.72 = (f32[128]{0:T(128)}, f32[128]{0:T(128)S(1)}, u32[]{:S(2)}) copy-start(f32[128]{0:T(128)S(1)} %broadcast_multiply_fusion.6) | copy-start | bytes 1540
  150.3 19.7 %copy-start.77 = (f32[128]{0:T(128)}, f32[128]{0:T(128)S(1)}, u32[]{:S(2)}) copy-start(f32[128]{0:T(128)S(1)} %add_rsqrt_fusion) | copy-start | bytes 1540
  150.3 37.2 %copy-start.90 = (bf16[768,768]{1,0:T(8,128)(2,1)S(1)}, bf16[768,768]{1,0:T(8,128)(2,1)}, u32[]{:S(2)}) copy-start(bf16[768,768]{1,0:T(8,128)(2,1)} %param.33) | copy-start | bytes 3538948
  195.3 97.6 %reduce-scatter.17.cloned.1.call-start = ((), (), s32[]{:S(2)}) async-start(), calls=%async_computation.11 | async-start | bytes 1966080 | tf_op jit(solution)/shard_map/reduce_scatter | solution.py:74
  231.8 21.6 %copy-start.43 = (bf16[192,768]{1,0:T(8,128)(2,1)S(1)}, bf16[192,768]{1,0:T(8,128)(2,1)}, u32[]{:S(2)}) copy-start(bf16[192,768]{1,0:T(8,128)(2,1)} %param.29) | copy-start | bytes 884740
  234.1 19.7 %copy-start.40 = (bf16[192,384]{0,1:T(8,128)(2,1)S(1)}, bf16[192,384]{0,1:T(8,128)(2,1)}, u32[]{:S(2)}) copy-start(bf16[192,384]{0,1:T(8,128)(2,1)} %copy.75) | copy-start | bytes 442372
  258.1 99.6 %reduce-scatter.19.cloned.1.call-start = ((), (), s32[]{:S(2)}) async-start(), calls=%async_computation.12 | async-start | bytes 1966080 | tf_op jit(solution)/shard_map/reduce_scatter | solution.py:74
  292.9 22.7 %copy-start.47 = (bf16[192,768]{1,0:T(8,128)(2,1)S(1)}, bf16[192,768]{1,0:T(8,128)(2,1)}, u32[]{:S(2)}) copy-start(bf16[192,768]{1,0:T(8,128)(2,1)} %param.25) | copy-start | bytes 884740
  294.2 21.8 %copy-start.2 = (f32[3,512,512]{1,2,0:T(8,128)S(1)}, f32[3,512,512]{1,2,0:T(8,128)}, u32[]{:S(2)}) copy-start(f32[3,512,512]{1,2,0:T(8,128)} %copy-done.1) | copy-start | bytes 9437188
  323.0 71.7 %reduce-scatter.21.cloned.1.call-start = ((), (), s32[]{:S(2)}) async-start(), calls=%async_computation.13 | async-start | bytes 1966080 | tf_op jit(solution)/shard_map/reduce_scatter | solution.py:78
  327.0 121.8 %reduce-scatter.25.cloned.1.call-start = ((), (), s32[]{:S(2)}) async-start(), calls=%async_computation.15 | async-start | bytes 2949120
  334.1 23.6 %copy-start.75 = (f32[128]{0:T(128)S(1)}, f32[128]{0:T(128)}, u32[]{:S(2)}) copy-start(f32[128]{0:T(128)} %copy-done.74) | copy-start | bytes 1540
  334.2 23.6 %copy-start.80 = (f32[128]{0:T(128)S(1)}, f32[128]{0:T(128)}, u32[]{:S(2)}) copy-start(f32[128]{0:T(128)} %copy-done.79) | copy-start | bytes 1540
  335.8 23.9 %copy-start.19 = (f32[128,768]{1,0:T(8,128)S(1)}, f32[128,768]{1,0:T(8,128)}, u32[]{:S(2)}) copy-start(f32[128,768]{1,0:T(8,128)} %get-tuple-element.204) | copy-start | bytes 1179652
  336.9 24.9 %copy-start.37 = (f32[128,768]{1,0:T(8,128)S(1)}, f32[128,768]{1,0:T(8,128)}, u32[]{:S(2)}) copy-start(f32[128,768]{1,0:T(8,128)} %reduce-scatter.11.cloned.1.call-done) | copy-start | bytes 1179652
  336.9 24.9 %copy-start.67 = (f32[768]{0:T(1024)S(1)}, f32[768]{0:T(1024)}, u32[]{:S(2)}) copy-start(f32[768]{0:T(1024)} %copy-done.66) | copy-start | bytes 9220
  361.8 32.9 %copy-start.34 = (bf16[1,128,768]{2,1,0:T(8,128)(2,1)S(1)}, bf16[1,128,768]{2,1,0:T(8,128)(2,1)}, u32[]{:S(2)}) copy-start(bf16[1,128,768]{2,1,0:T(8,128)(2,1)} %param.23) | copy-start | bytes 589828
  362.6 33.9 %copy-start.87 = (s32[128]{0:T(128)S(1)}, s32[128]{0:T(128)}, u32[]{:S(2)}) copy-start(s32[128]{0:T(128)} %copy-done.86) | copy-start | bytes 1540
  401.7 71.4 %reduce-scatter.23.cloned.1.call-start = ((), (), s32[]{:S(2)}) async-start(), calls=%async_computation.14 | async-start | bytes 737280 | tf_op jit(solution)/shard_map/reduce_scatter | solution.py:275
  403.9 253.2 %all-reduce.4.cloned.1.call-start = ((), (), s32[]{:S(2)}) async-start(), calls=%async_computation.16 | async-start | bytes 25952256 | tf_op jit(solution)/shard_map/psum | solution.py:82
  409.1 41.0 %copy-start.64 = (f32[1,3,768]{2,0,1:T(1,128)S(1)}, f32[1,3,768]{2,0,1:T(1,128)}, u32[]{:S(2)}) copy-start(f32[1,3,768]{2,0,1:T(1,128)} %param.20) | copy-start | bytes 27652
  452.8 39.4 %copy-start.82 = (f32[768]{0:T(1024)S(1)}, f32[768]{0:T(1024)}, u32[]{:S(2)}) copy-start(f32[768]{0:T(1024)} %get-tuple-element.201) | copy-start | bytes 9220
  (72 other events, 325.8 us)
Sparse Core Ops, SparseCore 0:
  53.7 36.0 reduce-scatter.10
  114.3 34.5 reduce-scatter.12
  195.4 34.8 reduce-scatter.14
  258.2 34.6 reduce-scatter.16
  323.1 34.5 reduce-scatter.18
  360.4 34.2 reduce-scatter.20
  401.8 46.9 reduce-scatter.24
  451.7 21.3 reduce-scatter.22
  479.0 178.0 all-reduce.3
